TPU v7x, 512 devices: a whole 4x8x8 slice. The times are simulated.
512 devices in a mesh: dp: 8 (over z), expert: 64 (over y, x, core).
Axes of the slice: x: 4, y: 8, z: 8, core: 2. Of those that a mesh axis runs over, the one named last changes fastest.
Arguments:
- tokens: bfloat16 [65536, 3584], P(('dp', 'expert')), may hold values from -6 to 6
- cotangent: bfloat16 [65536, 3584], P(('dp', 'expert')), may hold values from -6 to 6
- route_ids: int32 [65536, 8], P(('dp', 'expert')), may hold values from 0 to 255, as said below
- route_gates: float32 [65536, 8], P(('dp', 'expert')), may hold values from 0.1 to 1
- gate_w: bfloat16 [3584, 8192], P('dp', 'expert'), may hold values from -0.09375 to 0.09375
- up_w: bfloat16 [3584, 8192], P('dp', 'expert'), may hold values from -0.09375 to 0.09375
- down_w: bfloat16 [3584, 8192], P('dp', 'expert'), may hold values from -0.1875 to 0.1875
Outputs:
- moe_out: bfloat16 [65536, 3584], P(('dp', 'expert'))
- d_tokens: bfloat16 [65536, 3584], P(('dp', 'expert'))
- d_gates: float32 [65536, 8], P(('dp', 'expert'))
- d_gate_w: bfloat16 [3584, 8192], P('dp', 'expert')
- d_up_w: bfloat16 [3584, 8192], P('dp', 'expert')
- d_down_w: bfloat16 [3584, 8192], P('dp', 'expert')
Inputs may be any that keep to these rules, and one draw needn't show every extreme that they name: `route_ids`: each token names 8 different experts; the experts in flight are 0 to 7. Among the tokens of one device (aligned blocks of 128 tokens) each expert in flight is named by at most 6 tokens, and in every draw one expert in flight is named by exactly 6 tokens in every block.
All inputs are finite; a program needn't handle non-finite values.
Results may differ from a plain program's by a relative error of at most 0.017.
Values may be sent and summed in bfloat16 or wider, within the bound.
A program may use at most 64 MiB of HBM per device.

v0:
```python
import jax
import jax.numpy as jnp
from jax import lax
from jax.sharding import Mesh, PartitionSpec as P

SLICES = 8
CAP = 6
PAD = 8
BF = jnp.bfloat16
F32 = jnp.float32
CONTRACT_COLS = (((1,), (1,)), ((), ()))
CONTRACT_ROWS = (((0,), (0,)), ((), ()))


def dot(a, b, dims=(((1,), (0,)), ((), ()))):
    return lax.dot_general(a, b, dims, preferred_element_type=F32)


def routing(route_ids, route_gates, groups):
    tok_rows = route_ids.shape[0]
    experts = jnp.arange(groups, dtype=jnp.int32)
    match = route_ids[:, :, None] == experts[None, None, :]
    member = jnp.sum(match.astype(F32), axis=1)
    gate = jnp.sum(jnp.where(match, route_gates[:, :, None], 0.0), axis=1)
    row = lax.broadcasted_iota(jnp.int32, (tok_rows, tok_rows), 0)
    col = lax.broadcasted_iota(jnp.int32, (tok_rows, tok_rows), 1)
    before = (col < row).astype(BF)
    slot = dot(before, member.astype(BF))
    return (match, member, gate, slot)


def shards(tokens, cotangent, route_ids, route_gates, gate_w, up_w, down_w):
    groups = lax.axis_size("y")
    width = tokens.shape[1]
    tok_rows = tokens.shape[0]
    hid = gate_w.shape[1]
    match, member, gate, slot = routing(route_ids, route_gates, groups)
    wide = jnp.where(member > 0.5, slot, -1.0).T[:, None, :]
    sel = (wide == jnp.arange(PAD, dtype=F32)[None, :, None]).astype(F32)
    gates_t = gate.T[:, None, :]
    slot_gate = jnp.sum(sel * gates_t, axis=2)
    pick = sel.reshape(groups * PAD, tok_rows).astype(BF)
    token_slots = dot(pick, tokens).astype(BF)
    cot_slots = dot(pick, cotangent)
    scaled_slots = (slot_gate.reshape(groups * PAD, 1) * cot_slots).astype(BF)
    send = jnp.concatenate(
        [token_slots.reshape(groups, PAD, width), scaled_slots.reshape(groups, PAD, width)], axis=1
    )
    w_all = lax.all_gather(
        jnp.concatenate([gate_w, up_w, down_w], axis=1), "dp", axis=0, tiled=True
    )
    w_gate, w_up, w_down = (w_all[:, :hid], w_all[:, hid : 2 * hid], w_all[:, 2 * hid :])
    came = lax.all_to_all(send, "y", split_axis=0, concat_axis=0, tiled=True)
    rows = groups * CAP
    out_row = lax.broadcasted_iota(jnp.int32, (2 * rows, groups * 2 * PAD), 0)
    in_row = lax.broadcasted_iota(jnp.int32, (2 * rows, groups * 2 * PAD), 1)
    kind = (out_row >= rows).astype(jnp.int32)
    local = out_row - kind * rows
    wanted = local // CAP * (2 * PAD) + kind * PAD + local % CAP
    squeeze = (in_row == wanted).astype(BF)
    compact = dot(squeeze, came.reshape(groups * 2 * PAD, width)).astype(BF)
    both = lax.all_gather(compact, ("x", "c"), axis=0, tiled=False)
    n_slices = both.shape[0]
    token_rows = both[:, :rows].reshape(n_slices * rows, width)
    scaled_rows = both[:, rows:].reshape(n_slices * rows, width)
    gate_pre = dot(token_rows, w_gate)
    up_pre = dot(token_rows, w_up)
    sig = jax.nn.sigmoid(gate_pre)
    active = gate_pre * sig
    hidden = (active * up_pre).astype(BF)
    d_hidden = dot(scaled_rows, w_down)
    d_gate_pre = (d_hidden * up_pre * sig * (1.0 + gate_pre * (1.0 - sig))).astype(BF)
    d_up_pre = (d_hidden * active).astype(BF)
    out_part = dot(hidden, w_down, CONTRACT_COLS).astype(BF)
    dx_part = (dot(d_gate_pre, w_gate, CONTRACT_COLS) + dot(d_up_pre, w_up, CONTRACT_COLS)).astype(
        BF
    )
    parts = jnp.concatenate(
        [out_part.reshape(n_slices, rows, width), dx_part.reshape(n_slices, rows, width)], axis=1
    ).reshape(n_slices * 2 * rows, width)
    summed = lax.psum_scatter(parts, ("x", "c"), scatter_dimension=0, tiled=True)
    grads = jnp.concatenate(
        [
            dot(token_rows, d_gate_pre, CONTRACT_ROWS),
            dot(token_rows, d_up_pre, CONTRACT_ROWS),
            dot(scaled_rows, hidden, CONTRACT_ROWS),
        ],
        axis=1,
    ).astype(BF)
    grads = lax.psum_scatter(grads, "dp", scatter_dimension=0, tiled=True)
    back = dot(squeeze, summed, CONTRACT_ROWS).astype(BF).reshape(groups, 2 * PAD, width)
    back = lax.all_to_all(back, "y", split_axis=0, concat_axis=0, tiled=True)
    back = back.reshape(groups * 2 * PAD, width)
    zero = jnp.zeros_like(sel)
    member_out = jnp.concatenate([sel, zero], axis=1).reshape(groups * 2 * PAD, tok_rows)
    member_dx = jnp.concatenate([zero, sel], axis=1).reshape(groups * 2 * PAD, tok_rows)
    weight = jnp.concatenate([sel * gates_t, zero], axis=1).reshape(groups * 2 * PAD, tok_rows)
    high = weight.astype(BF)
    low = (weight - high.astype(F32)).astype(BF)
    moe_out = (dot(high, back, CONTRACT_ROWS) + dot(low, back, CONTRACT_ROWS)).astype(BF)
    d_tokens = dot(member_dx.astype(BF), back, CONTRACT_ROWS).astype(BF)
    inner = dot(back, cotangent, CONTRACT_COLS) * member_out
    by_expert = jnp.sum(inner.reshape(groups, 2 * PAD, tok_rows), axis=1).T
    d_gates = jnp.sum(jnp.where(match, by_expert[:, None, :], 0.0), axis=2)
    return (
        moe_out,
        d_tokens,
        d_gates,
        grads[:, :hid],
        grads[:, hid : 2 * hid],
        grads[:, 2 * hid :],
    )


def solution(mesh):
    dp, owners = mesh.devices.shape
    y = owners // SLICES
    grid = Mesh(mesh.devices.reshape(dp, y, SLICES // 2, 2), ("dp", "y", "x", "c"))
    rows = P(("dp", "y", "x", "c"), None)
    cols = P("dp", ("y", "x", "c"))
    return jax.shard_map(
        shards,
        mesh=grid,
        in_specs=(rows, rows, rows, rows, cols, cols, cols),
        out_specs=(rows, rows, rows, cols, cols, cols),
        check_vma=False,
    )
```

profile of v0, /device:TPU:2, one launch (start us, length us, event | category | flops | bytes accessed | tf_op | source)
XLA Modules:
  0.0 255.6 jit_solution(2671036714309216586)
XLA Ops:
  7.2 0.0 copy-start
  7.2 0.8 convert_reduce_fusion
  8.0 0.1 convolution_select_fusion
  8.1 0.1 fusion.22
  8.2 0.1 mul.76
  8.3 0.1 eq.53
  8.4 1.5 fusion.6
  9.9 0.0 copy-done
  9.9 0.3 fusion.5
  10.3 0.0 copy-start.5
  10.3 0.0 copy-start.6
  10.3 0.0 copy-start.7
  10.3 1.0 pad_maximum_fusion.2
  11.3 7.1 %all-to-all-start = ((bf16[8,16,3584]{2,1,0:T(8,128)(2,1)}), bf16[8,16,3584]{2,1,0:T(8,128)(2,1)S(1)}, u32[]{:S(2)}, u32[]{:S(2)}) async-start(bf16[8,16,3584]{2,1,0:T(8,128)(2,1)} %pad_maximum_fusion.2), calls=%async_computation | async-start | bytes 1835008 | tf_op jit(solution)/shard_map/all_to_all | solution.py:53
  18.4 0.0 all-gather.6.cloned.1.call-start
  18.5 25.8 %all-to-all-done = bf16[8,16,3584]{2,1,0:T(8,128)(2,1)S(1)} async-done(((bf16[8,16,3584]{2,1,0:T(8,128)(2,1)}), bf16[8,16,3584]{2,1,0:T(8,128)(2,1)S(1)}, u32[]{:S(2)}, u32[]{:S(2)}) %all-to-all-start) | async-done | bytes 917536 | tf_op jit(solution)/shard_map/all_to_all | solution.py:53
  44.3 1.3 convolution_convert_fusion.5
  45.6 0.0 all-gather.6.cloned.1.call-update
  45.6 0.0 all-gather.4.cloned.1.call-start
  45.7 0.0 copy-done.5
  45.7 0.0 copy-done.6
  45.7 0.0 copy-done.7
  45.7 0.8 pad_maximum_fusion.3
  46.5 0.0 all-gather.4.cloned.1.call-update
  46.5 0.0 reduce-scatter.5.cloned.1.call-start
  46.5 40.6 %all-gather.6.cloned.1.call-done = bf16[768,3584]{1,0:T(8,128)(2,1)} async-done(((bf16[96,3584]{1,0:T(8,128)(2,1)}), bf16[768,3584]{1,0:T(8,128)(2,1)}) %all-gather.6.cloned.1.call-update) | async-done | bytes 5505040 | tf_op jit(solution)/shard_map/all_gather | solution.py:62
  87.2 5.5 %fusion.33 = (bf16[8,48,3584]{2,1,0:T(8,128)(2,1)}, bf16[8,48,3584]{2,1,0:T(8,128)(2,1)}) fusion(bf16[8,96,3584]{2,1,0:T(8,128)(2,1)} %bitcast.70), kind=kLoop, calls=%fused_computation.75 | loop fusion | bytes 11010048 | tf_op jit(solution)/shard_map/slice | solution.py:65
  92.6 44.5 %all-gather.4.cloned.1.call-done = bf16[3584,384]{1,0:T(8,128)(2,1)} async-done(((bf16[448,384]{1,0:T(8,128)(2,1)}), bf16[3584,384]{1,0:T(8,128)(2,1)}) %all-gather.4.cloned.1.call-update) | async-done | bytes 2752528 | tf_op jit(solution)/shard_map/all_gather | solution.py:49
  137.1 0.0 copy-start.3
  137.1 0.0 copy-start.4
  137.1 3.0 %fusion.15 = f32[384,128]{1,0:T(8,128)S(1)} fusion(bf16[384,3584]{1,0:T(8,128)(2,1)} %bitcast.60, bf16[3584,384]{1,0:T(8,128)(2,1)} %all-gather.4.cloned.1.call-done), kind=kOutput, calls=%fused_computation.32 | convolution fusion | flops 352321536 | bytes 3866624 | tf_op jit(solution)/shard_map/dot_general | solution.py:16
  140.2 0.0 copy-start.1
  140.2 0.0 copy-done.3
  140.2 2.2 fusion.7
  142.4 0.0 copy-done.4
  142.4 0.0 copy-done.1
  142.4 0.9 multiply_convert_fusion.2
  143.3 0.9 fusion.13
  144.2 0.9 convolution_convert_fusion
  145.0 0.9 fusion
  145.9 2.8 %pad_maximum_fusion = bf16[8,96,3584]{2,1,0:T(8,128)(2,1)} fusion(bf16[8,48,3584]{2,1,0:T(8,128)(2,1)S(1)} %bitcast.69, bf16[8,48,3584]{2,1,0:T(8,128)(2,1)S(1)} %bitcast.68), kind=kLoop, calls=%fused_computation.3 | loop fusion | flops 11010048 | bytes 11010048 | tf_op jit(solution)/shard_map/concatenate | solution.py:78
  148.7 0.0 reduce-scatter.5.cloned.1.call-update
  148.7 0.0 reduce-scatter.7.cloned.1.call-start
  148.8 0.0 copy-start.2
  148.8 2.6 %convolution_convert_fusion.1 = bf16[3584,128]{0,1:T(8,128)(2,1)S(1)} fusion(bf16[384,3584]{1,0:T(8,128)(2,1)} %bitcast.66, bf16[384,128]{1,0:T(8,128)(2,1)S(1)} %get-tuple-element.28), kind=kOutput, calls=%fused_computation.10 | convolution fusion | flops 352780288 | bytes 3768320 | tf_op jit(solution)/shard_map/dot_general | solution.py:16
  151.4 0.0 copy-done.2
  151.4 0.7 convolution_convert_fusion.2
  152.1 0.7 convolution_convert_fusion.3
  152.8 1.8 pad_maximum_fusion.1
  154.6 4.5 %copy.27 = bf16[3584,384]{1,0:T(8,128)(2,1)} copy(bf16[3584,384]{0,1:T(8,128)(2,1)} %pad_maximum_fusion.1) | data formatting | bytes 5505024
  159.1 0.0 reduce-scatter.7.cloned.1.call-update
  159.2 0.0 copy-start.8
  159.2 30.2 %reduce-scatter.5.cloned.1.call-done = bf16[96,3584]{1,0:T(8,128)(2,1)} async-done(((bf16[768,3584]{1,0:T(8,128)(2,1)}), bf16[96,3584]{1,0:T(8,128)(2,1)}) %reduce-scatter.5.cloned.1.call-update) | async-done | bytes 688144 | tf_op jit(solution)/shard_map/reduce_scatter | solution.py:81
  189.3 2.6 %convolution_convert_fusion.4 = bf16[128,3584]{1,0:T(8,128)(2,1)} fusion(bf16[96,3584]{1,0:T(8,128)(2,1)} %reduce-scatter.5.cloned.1.call-done, s32[96]{0:T(128)S(1)} %broadcast_remainder_fusion, s32[96]{0:T(128)S(1)} %get-tuple-element.42, s32[96]{0:T(128)S(1)} %get-tuple-element.40, s32[96]{0:T(128)S(1)} %get-tuple-element.43, ...), kind=kOutput, calls=%fused_computation.13 | convolution fusion | flops 88612864 | bytes 1607744 | tf_op jit(solution)/shard_map/dot_general | solution.py:16
  191.9 6.8 %all-to-all-start.1 = ((bf16[8,16,3584]{2,1,0:T(8,128)(2,1)}), bf16[8,16,3584]{2,1,0:T(8,128)(2,1)S(1)}, u32[]{:S(2)}, u32[]{:S(2)}) async-start(bf16[8,16,3584]{2,1,0:T(8,128)(2,1)} %bitcast.12), calls=%async_computation.2 | async-start | bytes 1835008 | tf_op jit(solution)/shard_map/all_to_all | solution.py:92
  198.8 44.4 %reduce-scatter.7.cloned.1.call-done = bf16[448,384]{1,0:T(8,128)(2,1)} async-done(((bf16[3584,384]{1,0:T(8,128)(2,1)}), bf16[448,384]{1,0:T(8,128)(2,1)}) %reduce-scatter.7.cloned.1.call-update) | async-done | bytes 344080
  243.2 1.7 fusion.34
  245.0 0.0 all-to-all-done.1
  245.0 0.4 bitcast_reduce_fusion
  245.4 0.0 copy-done.8
  245.4 0.6 select_reduce_fusion
  246.0 0.4 convolution_bitcast_fusion.1
  246.4 1.4 fusion.2
  247.8 1.3 fusion.3
  (7 shorter events, 0.1 us)
Async XLA Ops:
  7.2 2.8 %copy-start = (bf16[128,3584]{1,0:T(8,128)(2,1)S(1)}, bf16[128,3584]{1,0:T(8,128)(2,1)}, u32[]{:S(2)}) copy-start(bf16[128,3584]{1,0:T(8,128)(2,1)} %param.8) | copy-start | bytes 2752516
  10.3 35.4 %copy-start.5 = (bf16[448,128]{1,0:T(8,128)(2,1)S(1)}, bf16[448,128]{1,0:T(8,128)(2,1)}, u32[]{:S(2)}) copy-start(bf16[448,128]{1,0:T(8,128)(2,1)} %param.13) | copy-start | bytes 344068
  10.3 35.4 %copy-start.6 = (bf16[448,128]{1,0:T(8,128)(2,1)S(1)}, bf16[448,128]{1,0:T(8,128)(2,1)}, u32[]{:S(2)}) copy-start(bf16[448,128]{1,0:T(8,128)(2,1)} %param.12) | copy-start | bytes 344068
  10.3 35.4 %copy-start.7 = (bf16[448,128]{1,0:T(8,128)(2,1)S(1)}, bf16[448,128]{1,0:T(8,128)(2,1)}, u32[]{:S(2)}) copy-start(bf16[448,128]{1,0:T(8,128)(2,1)} %param.11) | copy-start | bytes 344068
  11.3 33.0 %all-to-all-start = ((bf16[8,16,3584]{2,1,0:T(8,128)(2,1)}), bf16[8,16,3584]{2,1,0:T(8,128)(2,1)S(1)}, u32[]{:S(2)}, u32[]{:S(2)}) async-start(bf16[8,16,3584]{2,1,0:T(8,128)(2,1)} %pad_maximum_fusion.2), calls=%async_computation | async-start | bytes 1835008 | tf_op jit(solution)/shard_map/all_to_all | solution.py:53
  18.4 68.8 %all-gather.6.cloned.1.call-start = ((), (), s32[]{:S(2)}) async-start(), calls=%async_computation.6 | async-start | bytes 6193152 | tf_op jit(solution)/shard_map/all_gather | solution.py:62
  45.6 91.5 %all-gather.4.cloned.1.call-start = ((), (), s32[]{:S(2)}) async-start(), calls=%async_computation.4 | async-start | bytes 3096576 | tf_op jit(solution)/shard_map/all_gather | solution.py:49
  46.5 142.8 %reduce-scatter.5.cloned.1.call-start = ((), (), s32[]{:S(2)}) async-start(), calls=%async_computation.5 | async-start | bytes 6193152 | tf_op jit(solution)/shard_map/reduce_scatter | solution.py:81
  137.1 3.0 %copy-start.3 = (bf16[8,48,3584]{2,1,0:T(8,128)(2,1)S(1)}, bf16[8,48,3584]{2,1,0:T(8,128)(2,1)}, u32[]{:S(2)}) copy-start(bf16[8,48,3584]{2,1,0:T(8,128)(2,1)} %get-tuple-element.26) | copy-start | bytes 8257540
  137.1 5.3 %copy-start.4 = (bf16[3584,384]{1,0:T(8,128)(2,1)S(1)}, bf16[3584,384]{1,0:T(8,128)(2,1)}, u32[]{:S(2)}) copy-start(bf16[3584,384]{1,0:T(8,128)(2,1)} %all-gather.4.cloned.1.call-done) | copy-start | bytes 8257540
  140.2 2.2 copy-start.1
  148.7 94.5 %reduce-scatter.7.cloned.1.call-start = ((), (), s32[]{:S(2)}) async-start(), calls=%async_computation.7 | async-start | bytes 3096576
  148.8 2.6 %copy-start.2 = (bf16[8,48,3584]{2,1,0:T(8,128)(2,1)S(1)}, bf16[8,48,3584]{2,1,0:T(8,128)(2,1)}, u32[]{:S(2)}) copy-start(bf16[8,48,3584]{2,1,0:T(8,128)(2,1)} %get-tuple-element.27) | copy-start | bytes 8257540
  159.2 86.2 %copy-start.8 = (s32[128,8]{0,1:T(8,128)S(1)}, s32[128,8]{0,1:T(8,128)}, u32[]{:S(2)}) copy-start(s32[128,8]{0,1:T(8,128)} %param.9) | copy-start | bytes 12292
  191.9 53.0 %all-to-all-start.1 = ((bf16[8,16,3584]{2,1,0:T(8,128)(2,1)}), bf16[8,16,3584]{2,1,0:T(8,128)(2,1)S(1)}, u32[]{:S(2)}, u32[]{:S(2)}) async-start(bf16[8,16,3584]{2,1,0:T(8,128)(2,1)} %bitcast.12), calls=%async_computation.2 | async-start | bytes 1835008 | tf_op jit(solution)/shard_map/all_to_all | solution.py:92
Sparse Core Ops, SparseCore 0:
  45.7 41.3 all-gather.5
  89.8 47.2 all-gather.3
  148.8 40.4 reduce-scatter.4
  192.0 51.1 reduce-scatter.6
where the time goes:
time: 256 us
  waiting for transfers between devices  186 us (73%)
  matrix products  22.1 us (9%)
  starting transfers between devices  14.1 us (6%)
  between operations  14 us (5%)
  local copies, waits for them, and re-layouts  12 us (5%)
  other arithmetic  7.87 us (3%)
    unnamed x5, waiting for transfers between devices  44.5 us
    all_gather x1, waiting for transfers between devices, shards(): lax.all_gather(jnp.concatenate([gate_w, up_w, down_w], axis=1), 'dp', axi...  44.5 us
    all_gather x1, waiting for transfers between devices, shards(): both = lax.all_gather(compact, ('x', 'c'), axis=0, tiled=False)  40.6 us
    reduce_scatter x1, waiting for transfers between devices, shards(): lax.psum_scatter(parts, ('x', 'c'), scatter_dimension=0, tiled=True)  30.2 us
    all_to_all x1, waiting for transfers between devices, shards(): came = lax.all_to_all(send, 'y', split_axis=0, concat_axis=0, tiled=True)  25.8 us
    dot_general x18, matrix products, dot(): return lax.dot_general(a, b, dims, preferred_element_type=F32)  22.1 us
    all_to_all x1, starting transfers between devices, shards(): came = lax.all_to_all(send, 'y', split_axis=0, concat_axis=0, tiled=True)  7.09 us
    all_to_all x1, starting transfers between devices, shards(): back = lax.all_to_all(back, 'y', split_axis=0, concat_axis=0, tiled=True)  6.82 us
  transfers between devices with their start and end apart: 6, of which 5 were waited for; matrix products, arithmetic and copies ran while one was open for 8% of the time, Pallas kernels for 0%

commit v1 on v0

--- a/solution.py
+++ b/solution.py
@@ -10,6 +10,22 @@
 F32 = jnp.float32
 CONTRACT_COLS = (((1,), (1,)), ((), ()))
 CONTRACT_ROWS = (((0,), (0,)), ((), ()))
+
+
+def gather_around(x, axis, dim):
+    ways, here, step = (lax.axis_size(axis), lax.axis_index(axis), x.shape[dim])
+    lengths = [n * ways if d == dim else n for d, n in enumerate(x.shape)]
+    full = lax.dynamic_update_slice_in_dim(jnp.zeros(lengths, x.dtype), x, here * step, axis=dim)
+    going_up = going_down = x
+    for far in range(1, ways // 2 + 1):
+        going_up = lax.ppermute(going_up, axis, [(d, (d + 1) % ways) for d in range(ways)])
+        full = lax.dynamic_update_slice_in_dim(full, going_up, (here - far) % ways * step, axis=dim)
+        if 2 * far < ways:
+            going_down = lax.ppermute(going_down, axis, [(d, (d - 1) % ways) for d in range(ways)])
+            full = lax.dynamic_update_slice_in_dim(
+                full, going_down, (here + far) % ways * step, axis=dim
+            )
+    return full
 
 
 def dot(a, b, dims=(((1,), (0,)), ((), ()))):
@@ -46,9 +62,7 @@
     send = jnp.concatenate(
         [token_slots.reshape(groups, PAD, width), scaled_slots.reshape(groups, PAD, width)], axis=1
     )
-    w_all = lax.all_gather(
-        jnp.concatenate([gate_w, up_w, down_w], axis=1), "dp", axis=0, tiled=True
-    )
+    w_all = gather_around(jnp.concatenate([gate_w, up_w, down_w], axis=1), "dp", 0)
     w_gate, w_up, w_down = (w_all[:, :hid], w_all[:, hid : 2 * hid], w_all[:, 2 * hid :])
     came = lax.all_to_all(send, "y", split_axis=0, concat_axis=0, tiled=True)
     rows = groups * CAP

time: 256 us -> 222 us (0.87)
  the two profiles are of different devices: /device:TPU:2 before, /device:TPU:10 now
where the time goes in v1:
time: 222 us; the launch traced here: 221 us
  waiting for transfers between devices  112 us (50%)
  starting transfers between devices  44 us (20%)
  matrix products  26.5 us (12%)
  local copies, waits for them, and re-layouts  17.5 us (8%)
  between operations  14.2 us (6%)
  other arithmetic  7.02 us (3%)
    unnamed x4, waiting for transfers between devices  44.3 us
    reduce_scatter x1, waiting for transfers between devices, shards(): lax.psum_scatter(parts, ('x', 'c'), scatter_dimension=0, tiled=True)  31.9 us
    dot_general x18, matrix products, dot(): return lax.dot_general(a, b, dims, preferred_element_type=F32)  26.5 us
    all_to_all x1, waiting for transfers between devices, shards(): came = lax.all_to_all(send, 'y', split_axis=0, concat_axis=0, tiled=True)  24.4 us
    ppermute x3, starting transfers between devices, gather_around(): lax.ppermute(going_down, axis, [(d, (d - 1) % ways) for d in range(ways)])  18.9 us
    ppermute x4, waiting for transfers between devices, gather_around(): lax.ppermute(going_up, axis, [(d, (d + 1) % ways) for d in range(ways)])  11.4 us
    ppermute x4, starting transfers between devices, gather_around(): lax.ppermute(going_up, axis, [(d, (d + 1) % ways) for d in range(ways)])  10 us
    all_to_all x1, starting transfers between devices, shards(): came = lax.all_to_all(send, 'y', split_axis=0, concat_axis=0, tiled=True)  7.68 us
  transfers between devices with their start and end apart: 12, of which 7 were waited for; matrix products, arithmetic and copies ran while one was open for 10% of the time, Pallas kernels for 0%

profile of v1, /device:TPU:10, one launch (start us, length us, event | category | flops | bytes accessed | tf_op | source)
XLA Modules:
  0.0 221.2 jit_solution(16458480490275799446)
XLA Ops:
  7.2 0.0 copy-start
  7.2 0.8 convert_reduce_fusion
  8.0 0.1 convolution_select_fusion
  8.1 0.1 fusion.22
  8.2 0.1 mul.100
  8.3 0.1 eq.61
  8.4 1.5 fusion.6
  9.9 0.3 fusion.5
  10.3 0.0 copy-start.4
  10.3 0.0 copy-start.5
  10.3 1.0 pad_maximum_fusion.2
  11.3 7.7 %all-to-all-start = ((bf16[8,16,3584]{2,1,0:T(8,128)(2,1)}), bf16[8,16,3584]{2,1,0:T(8,128)(2,1)S(1)}, u32[]{:S(2)}, u32[]{:S(2)}) async-start(bf16[8,16,3584]{2,1,0:T(8,128)(2,1)} %pad_maximum_fusion.2), calls=%async_computation | async-start | bytes 1835008 | tf_op jit(solution)/shard_map/all_to_all | solution.py:67
  19.0 24.4 %all-to-all-done = bf16[8,16,3584]{2,1,0:T(8,128)(2,1)S(1)} async-done(((bf16[8,16,3584]{2,1,0:T(8,128)(2,1)}), bf16[8,16,3584]{2,1,0:T(8,128)(2,1)S(1)}, u32[]{:S(2)}, u32[]{:S(2)}) %all-to-all-start) | async-done | bytes 917536 | tf_op jit(solution)/shard_map/all_to_all | solution.py:67
  43.4 1.3 convolution_convert_fusion.5
  44.7 0.0 all-gather.3.cloned.1.call-update
  44.7 0.0 reduce-scatter.5.cloned.1.call-start
  44.9 4.3 %collective-permute-start = (bf16[448,384]{1,0:T(8,128)(2,1)S(1)}, bf16[448,384]{1,0:T(8,128)(2,1)S(1)}, u32[]{:S(2)}, u32[]{:S(2)}) collective-permute-start(bf16[448,384]{1,0:T(8,128)(2,1)S(1)} %constant_dynamic-update-slice_fusion), channel_id=1, source_target_pairs={{0,64},{64,128},{128,192},{192,256},{256,320},{320,384},{384,448},... | collective-permute-start | bytes 1032200 | tf_op jit(solution)/shard_map/ppermute | solution.py:21
  49.2 8.6 %collective-permute-start.1 = (bf16[448,384]{1,0:T(8,128)(2,1)S(1)}, bf16[448,384]{1,0:T(8,128)(2,1)S(1)}, u32[]{:S(2)}, u32[]{:S(2)}) collective-permute-start(bf16[448,384]{1,0:T(8,128)(2,1)S(1)} %constant_dynamic-update-slice_fusion), channel_id=1, source_target_pairs={{0,448},{64,0},{128,64},{192,128},{256,192},{320,256},{384,320},{4... | collective-permute-start | bytes 1032200 | tf_op jit(solution)/shard_map/ppermute | solution.py:24
  57.8 3.7 %collective-permute-done = bf16[448,384]{1,0:T(8,128)(2,1)S(1)} collective-permute-done((bf16[448,384]{1,0:T(8,128)(2,1)S(1)}, bf16[448,384]{1,0:T(8,128)(2,1)S(1)}, u32[]{:S(2)}, u32[]{:S(2)}) %collective-permute-start) | collective-permute-done | bytes 344096 | tf_op jit(solution)/shard_map/ppermute | solution.py:21
  61.5 1.9 collective-permute-start.2
  63.6 5.1 %collective-permute-start.3 = (bf16[448,384]{1,0:T(8,128)(2,1)S(1)}, bf16[448,384]{1,0:T(8,128)(2,1)S(1)}, u32[]{:S(2)}, u32[]{:S(2)}) collective-permute-start(bf16[448,384]{1,0:T(8,128)(2,1)S(1)} %collective-permute-done.1), channel_id=1, source_target_pairs={{0,448},{64,0},{128,64},{192,128},{256,192},{320,256},{384,320},{4... | collective-permute-start | bytes 1032200 | tf_op jit(solution)/shard_map/ppermute | solution.py:24
  68.7 1.8 broadcast_in_dim.40
  70.5 0.8 constant_dynamic-update-slice_fusion.10
  71.2 0.6 collective-permute-done.2
  71.8 1.9 collective-permute-start.4
  73.8 0.8 constant_dynamic-update-slice_fusion.9
  74.5 0.8 constant_dynamic-update-slice_fusion.8
  75.3 0.0 collective-permute-done.3
  75.3 5.1 %collective-permute-start.5 = (bf16[448,384]{1,0:T(8,128)(2,1)S(1)}, bf16[448,384]{1,0:T(8,128)(2,1)S(1)}, u32[]{:S(2)}, u32[]{:S(2)}) collective-permute-start(bf16[448,384]{1,0:T(8,128)(2,1)S(1)} %collective-permute-done.3), channel_id=1, source_target_pairs={{0,448},{64,0},{128,64},{192,128},{256,192},{320,256},{384,320},{4... | collective-permute-start | bytes 1032200 | tf_op jit(solution)/shard_map/ppermute | solution.py:24
  80.4 0.8 constant_dynamic-update-slice_fusion.7
  81.2 1.0 collective-permute-done.4
  82.2 1.9 collective-permute-start.6
  84.1 0.8 constant_dynamic-update-slice_fusion.6
  84.9 0.8 constant_dynamic-update-slice_fusion.5
  85.7 0.8 constant_dynamic-update-slice_fusion.4
  86.5 6.1 %collective-permute-done.6 = bf16[448,384]{1,0:T(8,128)(2,1)S(1)} collective-permute-done((bf16[448,384]{1,0:T(8,128)(2,1)S(1)}, bf16[448,384]{1,0:T(8,128)(2,1)S(1)}, u32[]{:S(2)}, u32[]{:S(2)}) %collective-permute-start.6) | collective-permute-done | bytes 344096 | tf_op jit(solution)/shard_map/ppermute | solution.py:21
  92.5 0.8 constant_dynamic-update-slice_fusion.3
  93.3 3.0 %fusion.33 = (bf16[8,48,3584]{2,1,0:T(8,128)(2,1)S(1)}, bf16[8,48,3584]{2,1,0:T(8,128)(2,1)S(1)}) fusion(bf16[8,96,3584]{2,1,0:T(8,128)(2,1)} %bitcast.70), kind=kLoop, calls=%fused_computation.85 | loop fusion | bytes 11010048 | tf_op jit(solution)/shard_map/slice | solution.py:78
  96.3 2.8 %fusion.7 = f32[384,128]{1,0:T(8,128)S(1)} fusion(bf16[384,3584]{1,0:T(8,128)(2,1)S(1)} %bitcast.66, bf16[3584,384]{1,0:T(8,128)(2,1)} %constant_dynamic-update-slice_fusion.3), kind=kOutput, calls=%fused_computation.24 | convolution fusion | flops 352321536 | bytes 3866624 | tf_op jit(solution)/shard_map/dot_general | solution.py:32
  99.0 2.1 fusion.15
  101.1 2.1 multiply_convert_fusion.2
  103.2 2.1 convolution_convert_fusion
  105.3 2.1 fusion.10
  107.3 2.1 fusion
  109.4 2.8 %pad_maximum_fusion = bf16[8,96,3584]{2,1,0:T(8,128)(2,1)} fusion(bf16[8,48,3584]{2,1,0:T(8,128)(2,1)S(1)} %bitcast.69, bf16[8,48,3584]{2,1,0:T(8,128)(2,1)S(1)} %bitcast.68), kind=kLoop, calls=%fused_computation.3 | loop fusion | flops 11010048 | bytes 11010048 | tf_op jit(solution)/shard_map/concatenate | solution.py:92
  112.2 0.0 reduce-scatter.5.cloned.1.call-update
  112.2 0.0 reduce-scatter.7.cloned.1.call-start
  112.3 2.6 %convolution_convert_fusion.1 = bf16[3584,128]{0,1:T(8,128)(2,1)S(1)} fusion(bf16[384,3584]{1,0:T(8,128)(2,1)} %bitcast.67, bf16[384,128]{1,0:T(8,128)(2,1)S(1)} %get-tuple-element.28), kind=kOutput, calls=%fused_computation.10 | convolution fusion | flops 352780288 | bytes 3768320 | tf_op jit(solution)/shard_map/dot_general | solution.py:32
  114.9 0.7 convolution_convert_fusion.2
  115.6 0.7 convolution_convert_fusion.3
  116.3 1.7 pad_maximum_fusion.1
  118.0 4.5 %copy.27 = bf16[3584,384]{1,0:T(8,128)(2,1)} copy(bf16[3584,384]{0,1:T(8,128)(2,1)} %pad_maximum_fusion.1) | data formatting | bytes 5505024
  122.5 0.0 reduce-scatter.7.cloned.1.call-update
  122.6 0.0 copy-start.7
  122.6 31.9 %reduce-scatter.5.cloned.1.call-done = bf16[96,3584]{1,0:T(8,128)(2,1)} async-done(((bf16[768,3584]{1,0:T(8,128)(2,1)}), bf16[96,3584]{1,0:T(8,128)(2,1)}) %reduce-scatter.5.cloned.1.call-update) | async-done | bytes 688144 | tf_op jit(solution)/shard_map/reduce_scatter | solution.py:95
  154.5 2.6 %convolution_convert_fusion.4 = bf16[128,3584]{1,0:T(8,128)(2,1)} fusion(bf16[96,3584]{1,0:T(8,128)(2,1)} %reduce-scatter.5.cloned.1.call-done, s32[96]{0:T(128)S(1)} %broadcast_remainder_fusion, s32[96]{0:T(128)S(1)} %get-tuple-element.42, s32[96]{0:T(128)S(1)} %get-tuple-element.40, s32[96]{0:T(128)S(1)} %get-tuple-element.43, ...), kind=kOutput, calls=%fused_computation.13 | convolution fusion | flops 88612864 | bytes 1607744 | tf_op jit(solution)/shard_map/dot_general | solution.py:32
  157.1 7.4 %all-to-all-start.1 = ((bf16[8,16,3584]{2,1,0:T(8,128)(2,1)}), bf16[8,16,3584]{2,1,0:T(8,128)(2,1)S(1)}, u32[]{:S(2)}, u32[]{:S(2)}) async-start(bf16[8,16,3584]{2,1,0:T(8,128)(2,1)} %bitcast.12), calls=%async_computation.2 | async-start | bytes 1835008 | tf_op jit(solution)/shard_map/all_to_all | solution.py:106
  164.5 44.2 %reduce-scatter.7.cloned.1.call-done = bf16[448,384]{1,0:T(8,128)(2,1)} async-done(((bf16[3584,384]{1,0:T(8,128)(2,1)}), bf16[448,384]{1,0:T(8,128)(2,1)}) %reduce-scatter.7.cloned.1.call-update) | async-done | bytes 344080
  208.7 1.7 fusion.34
  210.5 0.4 bitcast_reduce_fusion
  210.9 0.6 select_reduce_fusion
  211.5 0.4 convolution_bitcast_fusion.1
  211.9 1.4 fusion.2
  213.3 1.3 fusion.3
  (27 shorter events, 0.2 us)
Async XLA Ops:
  7.2 2.7 %copy-start = (bf16[128,3584]{1,0:T(8,128)(2,1)S(1)}, bf16[128,3584]{1,0:T(8,128)(2,1)}, u32[]{:S(2)}) copy-start(bf16[128,3584]{1,0:T(8,128)(2,1)} %param.8) | copy-start | bytes 2752516
  10.3 34.5 %copy-start.4 = (bf16[448,128]{1,0:T(8,128)(2,1)S(1)}, bf16[448,128]{1,0:T(8,128)(2,1)}, u32[]{:S(2)}) copy-start(bf16[448,128]{1,0:T(8,128)(2,1)} %param.11) | copy-start | bytes 344068
  10.3 34.5 %copy-start.5 = (bf16[448,128]{1,0:T(8,128)(2,1)S(1)}, bf16[448,128]{1,0:T(8,128)(2,1)}, u32[]{:S(2)}) copy-start(bf16[448,128]{1,0:T(8,128)(2,1)} %param.12) | copy-start | bytes 344068
  11.3 33.6 %copy-start.6 = (bf16[448,128]{1,0:T(8,128)(2,1)S(1)}, bf16[448,128]{1,0:T(8,128)(2,1)}, u32[]{:S(2)}) copy-start(bf16[448,128]{1,0:T(8,128)(2,1)} %param.13) | copy-start | bytes 344068
  11.3 32.1 %all-to-all-start = ((bf16[8,16,3584]{2,1,0:T(8,128)(2,1)}), bf16[8,16,3584]{2,1,0:T(8,128)(2,1)S(1)}, u32[]{:S(2)}, u32[]{:S(2)}) async-start(bf16[8,16,3584]{2,1,0:T(8,128)(2,1)} %pad_maximum_fusion.2), calls=%async_computation | async-start | bytes 1835008 | tf_op jit(solution)/shard_map/all_to_all | solution.py:67
  18.9 74.3 %all-gather.3.cloned.1.call-start = ((), (), s32[]{:S(2)}) async-start(), calls=%async_computation.5 | async-start | bytes 6193152 | tf_op jit(solution)/shard_map/all_gather | solution.py:76
  44.7 109.8 %reduce-scatter.5.cloned.1.call-start = ((), (), s32[]{:S(2)}) async-start(), calls=%async_computation.4 | async-start | bytes 6193152 | tf_op jit(solution)/shard_map/reduce_scatter | solution.py:95
  44.9 16.6 %collective-permute-start = (bf16[448,384]{1,0:T(8,128)(2,1)S(1)}, bf16[448,384]{1,0:T(8,128)(2,1)S(1)}, u32[]{:S(2)}, u32[]{:S(2)}) collective-permute-start(bf16[448,384]{1,0:T(8,128)(2,1)S(1)} %constant_dynamic-update-slice_fusion), channel_id=1, source_target_pairs={{0,64},{64,128},{128,192},{192,256},{256,320},{320,384},{384,448},... | collective-permute-start | bytes 1032200 | tf_op jit(solution)/shard_map/ppermute | solution.py:21
  49.2 14.4 %collective-permute-start.1 = (bf16[448,384]{1,0:T(8,128)(2,1)S(1)}, bf16[448,384]{1,0:T(8,128)(2,1)S(1)}, u32[]{:S(2)}, u32[]{:S(2)}) collective-permute-start(bf16[448,384]{1,0:T(8,128)(2,1)S(1)} %constant_dynamic-update-slice_fusion), channel_id=1, source_target_pairs={{0,448},{64,0},{128,64},{192,128},{256,192},{320,256},{384,320},{4... | collective-permute-start | bytes 1032200 | tf_op jit(solution)/shard_map/ppermute | solution.py:24
  61.5 10.3 %collective-permute-start.2 = (bf16[448,384]{1,0:T(8,128)(2,1)S(1)}, bf16[448,384]{1,0:T(8,128)(2,1)S(1)}, u32[]{:S(2)}, u32[]{:S(2)}) collective-permute-start(bf16[448,384]{1,0:T(8,128)(2,1)S(1)} %collective-permute-done), channel_id=1, source_target_pairs={{0,64},{64,128},{128,192},{192,256},{256,320},{320,384},{384,448},... | collective-permute-start | bytes 1032200 | tf_op jit(solution)/shard_map/ppermute | solution.py:21
  63.6 11.7 %collective-permute-start.3 = (bf16[448,384]{1,0:T(8,128)(2,1)S(1)}, bf16[448,384]{1,0:T(8,128)(2,1)S(1)}, u32[]{:S(2)}, u32[]{:S(2)}) collective-permute-start(bf16[448,384]{1,0:T(8,128)(2,1)S(1)} %collective-permute-done.1), channel_id=1, source_target_pairs={{0,448},{64,0},{128,64},{192,128},{256,192},{320,256},{384,320},{4... | collective-permute-start | bytes 1032200 | tf_op jit(solution)/shard_map/ppermute | solution.py:24
  71.8 10.3 %collective-permute-start.4 = (bf16[448,384]{1,0:T(8,128)(2,1)S(1)}, bf16[448,384]{1,0:T(8,128)(2,1)S(1)}, u32[]{:S(2)}, u32[]{:S(2)}) collective-permute-start(bf16[448,384]{1,0:T(8,128)(2,1)S(1)} %collective-permute-done.2), channel_id=1, source_target_pairs={{0,64},{64,128},{128,192},{192,256},{256,320},{320,384},{384,448},... | collective-permute-start | bytes 1032200 | tf_op jit(solution)/shard_map/ppermute | solution.py:21
  75.3 10.4 %collective-permute-start.5 = (bf16[448,384]{1,0:T(8,128)(2,1)S(1)}, bf16[448,384]{1,0:T(8,128)(2,1)S(1)}, u32[]{:S(2)}, u32[]{:S(2)}) collective-permute-start(bf16[448,384]{1,0:T(8,128)(2,1)S(1)} %collective-permute-done.3), channel_id=1, source_target_pairs={{0,448},{64,0},{128,64},{192,128},{256,192},{320,256},{384,320},{4... | collective-permute-start | bytes 1032200 | tf_op jit(solution)/shard_map/ppermute | solution.py:24
  82.2 10.3 %collective-permute-start.6 = (bf16[448,384]{1,0:T(8,128)(2,1)S(1)}, bf16[448,384]{1,0:T(8,128)(2,1)S(1)}, u32[]{:S(2)}, u32[]{:S(2)}) collective-permute-start(bf16[448,384]{1,0:T(8,128)(2,1)S(1)} %collective-permute-done.4), channel_id=1, source_target_pairs={{0,64},{64,128},{128,192},{192,256},{256,320},{320,384},{384,448},... | collective-permute-start | bytes 1032200 | tf_op jit(solution)/shard_map/ppermute | solution.py:21
  96.3 4.9 %copy-start.1 = (bf16[8,48,3584]{2,1,0:T(8,128)(2,1)}, bf16[8,48,3584]{2,1,0:T(8,128)(2,1)S(1)}, u32[]{:S(2)}) copy-start(bf16[8,48,3584]{2,1,0:T(8,128)(2,1)S(1)} %get-tuple-element.26) | copy-start | bytes 8257540
  96.3 4.9 %copy-start.3 = (bf16[8,48,3584]{2,1,0:T(8,128)(2,1)}, bf16[8,48,3584]{2,1,0:T(8,128)(2,1)S(1)}, u32[]{:S(2)}) copy-start(bf16[8,48,3584]{2,1,0:T(8,128)(2,1)S(1)} %get-tuple-element.27) | copy-start | bytes 8257540
  112.2 96.5 %reduce-scatter.7.cloned.1.call-start = ((), (), s32[]{:S(2)}) async-start(), calls=%async_computation.6 | async-start | bytes 3096576
  112.3 2.6 %copy-start.2 = (bf16[8,48,3584]{2,1,0:T(8,128)(2,1)S(1)}, bf16[8,48,3584]{2,1,0:T(8,128)(2,1)}, u32[]{:S(2)}) copy-start(bf16[8,48,3584]{2,1,0:T(8,128)(2,1)} %copy-done.1) | copy-start | bytes 8257540
  122.6 88.3 %copy-start.7 = (s32[128,8]{0,1:T(8,128)S(1)}, s32[128,8]{0,1:T(8,128)}, u32[]{:S(2)}) copy-start(s32[128,8]{0,1:T(8,128)} %param.9) | copy-start | bytes 12292
  157.1 53.4 %all-to-all-start.1 = ((bf16[8,16,3584]{2,1,0:T(8,128)(2,1)}), bf16[8,16,3584]{2,1,0:T(8,128)(2,1)S(1)}, u32[]{:S(2)}, u32[]{:S(2)}) async-start(bf16[8,16,3584]{2,1,0:T(8,128)(2,1)} %bitcast.12), calls=%async_computation.2 | async-start | bytes 1835008 | tf_op jit(solution)/shard_map/all_to_all | solution.py:106
Sparse Core Ops, SparseCore 0:
  44.8 42.2 all-gather.2
  112.3 42.1 reduce-scatter.4
  157.4 51.3 reduce-scatter.6
